TPU v7x, 32 devices: a whole 2x2x4 slice. The times are simulated.
32 devices in a mesh: ex: 2 (over core), ey: 16 (over z, y, x).
Axes of the slice: x: 2, y: 2, z: 4, core: 2. Of those that a mesh axis runs over, the one named last changes fastest.
Arguments:
- tokens: bfloat16 [32, 256, 1024], P(('ex', 'ey')), may hold values from -16 to 16
- slot_param: bfloat16 [1024, 32], replicated, may hold values from -0.75 to 0.75
- weight_in: bfloat16 [32, 1024, 4096], P('ey', None, 'ex'), may hold values from -0.1875 to 0.1875
- weight_out: bfloat16 [32, 4096, 1024], P('ey', 'ex'), may hold values from -0.09375 to 0.09375
- grad_out: bfloat16 [32, 256, 1024], P(('ex', 'ey')), may hold values from -6 to 6
Outputs:
- grad_tokens: bfloat16 [32, 256, 1024], P(('ex', 'ey'))
- grad_param: float32 [1024, 32], replicated
- grad_win: bfloat16 [32, 1024, 4096], P('ey', None, 'ex')
- grad_wout: bfloat16 [32, 4096, 1024], P('ey', 'ex')
All inputs are finite; a program needn't handle non-finite values.
Results may differ from a plain program's by a relative error of at most 0.017.
Values may be sent and summed in bfloat16 or wider, within the bound.
No kernel may reach another device: no remote copies, remote signals or barrier semaphores. Data moves between devices by JAX's collectives and lax.ppermute only.
A program may use at most 64 MiB of HBM per device.

v0:
```python
import jax
import jax.numpy as jnp
from jax import lax
from jax.sharding import PartitionSpec as P


def gelu_parts(pre):
    cdf = 0.5 * (1.0 + lax.erf(pre * 0.7071067811865476))
    slope = cdf + pre * jnp.exp(-0.5 * pre * pre) * 0.3989422804014327
    return (pre * cdf, slope)


def softmax_along(values, axis):
    top = jnp.max(values, axis=axis, keepdims=True)
    expo = jnp.exp(values - top)
    return expo / jnp.sum(expo, axis=axis, keepdims=True)


def route_in(stacked):
    moved = lax.all_to_all(stacked, "ey", split_axis=2, concat_axis=0, tiled=True)
    return lax.all_gather(moved, "ex", axis=0, tiled=True)


def route_out(term_fn, total_rows):
    summed = lax.psum_scatter(
        term_fn(jnp.int32(0), total_rows // lax.axis_size("ex") * lax.axis_size("ex")).astype(
            jnp.bfloat16
        ),
        "ex",
        scatter_dimension=0,
        tiled=True,
    )
    return lax.all_to_all(summed, "ey", split_axis=0, concat_axis=2, tiled=True)


def per_device(tokens, slot_param, weight_in, weight_out, grad_out):
    logits = jnp.einsum("ipd,ds->ips", tokens, slot_param, preferred_element_type=jnp.float32)
    dispatch = softmax_along(logits, 1)
    combine = softmax_along(logits, 2)
    dispatch_b = dispatch.astype(jnp.bfloat16)
    combine_b = combine.astype(jnp.bfloat16)
    slot_in = jnp.einsum(
        "ips,ipd->isd", dispatch_b, tokens, preferred_element_type=jnp.float32
    ).astype(jnp.bfloat16)
    slot_cot = jnp.einsum(
        "ips,ipd->isd", combine_b, grad_out, preferred_element_type=jnp.float32
    ).astype(jnp.bfloat16)
    arrived = route_in(jnp.stack((slot_in, slot_cot), axis=1))
    total_rows = arrived.shape[0]
    slot_x = arrived[:, 0]
    slot_g = arrived[:, 1]
    pre = jnp.einsum("red,edf->ref", slot_x, weight_in, preferred_element_type=jnp.float32)
    value, slope = gelu_parts(pre)
    hidden = value.astype(jnp.bfloat16)
    back = jnp.einsum("red,efd->ref", slot_g, weight_out, preferred_element_type=jnp.float32)
    dpre = (back * slope).astype(jnp.bfloat16)

    def paired_term(start, count):
        return jnp.concatenate(
            (
                jnp.einsum("ref,efd->red", hidden, weight_out, preferred_element_type=jnp.float32)[
                    :, None
                ],
                jnp.einsum("ref,edf->red", dpre, weight_in, preferred_element_type=jnp.float32)[
                    :, None
                ],
            ),
            axis=1,
        )

    paired = route_out(paired_term, total_rows)
    slot_out = paired[:, 0]
    grad_slot = paired[:, 1]
    grad_win = jnp.einsum("red,ref->edf", slot_x, dpre, preferred_element_type=jnp.float32).astype(
        jnp.bfloat16
    )
    grad_wout = jnp.einsum(
        "ref,red->efd", hidden, slot_g, preferred_element_type=jnp.float32
    ).astype(jnp.bfloat16)
    d_combine = jnp.einsum("ipd,isd->ips", grad_out, slot_out, preferred_element_type=jnp.float32)
    d_dispatch = jnp.einsum("ipd,isd->ips", tokens, grad_slot, preferred_element_type=jnp.float32)
    d_logits = dispatch * (d_dispatch - jnp.sum(dispatch * d_dispatch, axis=1, keepdims=True))
    d_logits = d_logits + combine * (
        d_combine - jnp.sum(combine * d_combine, axis=2, keepdims=True)
    )
    logit_grad = d_logits.astype(jnp.bfloat16)
    grad_tokens = jnp.einsum(
        "ips,isd->ipd", dispatch_b, grad_slot, preferred_element_type=jnp.float32
    )
    grad_tokens = grad_tokens + jnp.einsum(
        "ips,ds->ipd", logit_grad, slot_param, preferred_element_type=jnp.float32
    )
    local_param = jnp.einsum("ipd,ips->ds", tokens, logit_grad, preferred_element_type=jnp.float32)
    grad_param = lax.psum(local_param, ("ex", "ey"))
    return (grad_tokens.astype(jnp.bfloat16), grad_param, grad_win, grad_wout)


def solution(mesh):
    in_specs = (
        P(("ex", "ey"), None, None),
        P(),
        P("ey", None, "ex"),
        P("ey", "ex", None),
        P(("ex", "ey"), None, None),
    )
    out_specs = (P(("ex", "ey"), None, None), P(), P("ey", None, "ex"), P("ey", "ex", None))
    return jax.shard_map(
        per_device, mesh=mesh, in_specs=in_specs, out_specs=out_specs, check_vma=False
    )
```

profile of v0, /device:TPU:0, one launch (start us, length us, event | category | flops | bytes accessed | tf_op | source)
XLA Modules:
  0.0 198.2 jit_solution(10697608207090606354)
XLA Ops:
  7.2 0.0 copy-start
  7.2 0.0 reduce-scatter.2.cloned.1.call-start
  7.2 1.0 copy-done
  8.2 1.2 fusion.36
  9.4 0.2 fusion.25
  9.6 0.2 fusion.6
  9.9 1.2 fusion.7
  11.1 0.1 copy.17
  11.3 15.9 %all_to_all.36 = bf16[1,2,32,1024]{3,1,0,2:T(2,128)(2,1)S(1)} all-to-all(bf16[1,2,32,1024]{3,1,0,2:T(2,128)(2,1)S(1)} %copy.17), channel_id=1, replica_groups=mesh['ex'=2,'ey'=16] {'ey'}, dimensions={2} | all-to-all | bytes 262144 | tf_op jit(solution)/shard_map/all_to_all | solution.py:20
  27.2 0.0 slice-start
  27.3 2.1 %all-gather = bf16[32,1,2,2,1024]{4,0,3,2,1:T(8,128)(2,1)S(1)} all-gather(bf16[16,1,2,2,1024]{4,0,3,2,1:T(8,128)(2,1)S(1)} %bitcast.90), channel_id=2, replica_groups=mesh['ex'=2,'ey'=16] {'ex'}, dimensions={0}, use_global_device_ids=true | all-gather | bytes 393216 | tf_op jit(solution)/shard_map/all_gather | solution.py:21
  29.4 0.0 slice-start.1
  29.4 0.0 slice-start.2
  29.4 5.1 %convolution_bitcast_fusion.1 = f32[32,2,2048]{2,0,1:T(8,128)S(1)} fusion(bf16[2,1024,2048]{2,1,0:T(8,128)(2,1)} %param.7, bf16[32,2,2,1024]{3,0,2,1:T(8,128)(2,1)S(1)} %bitcast.85), kind=kOutput, calls=%fused_computation.4 | convolution fusion | flops 268435456 | bytes 9043968 | tf_op jit(solution)/shard_map/red,edf->ref/dot_general | solution.py:52
  34.5 0.0 slice-done
  34.5 0.0 slice-done.1
  34.5 0.0 slice-start.3
  34.5 1.5 fusion.4
  36.0 2.6 %fusion.1 = bf16[32,2,2048]{2,0,1:T(8,128)(2,1)S(1)} fusion(bf16[2,2048,1024]{2,1,0:T(8,128)(2,1)S(1)} %bitcast.82, f32[32,2,2048]{2,0,1:T(8,128)S(1)} %convolution_bitcast_fusion.1, bf16[32,2,2,1024]{3,0,2,1:T(8,128)(2,1)S(1)} %bitcast.86), kind=kOutput, calls=%fused_computation.5 | convolution fusion | flops 269746176 | bytes 9306112 | tf_op jit(solution)/shard_map/red,efd->ref/dot_general | solution.py:55
  38.6 0.0 slice-done.2
  38.7 0.0 slice-done.3
  38.7 2.6 %fusion.5 = bf16[32,1,2,1024]{3,0,2,1:T(8,128)(2,1)S(1)} fusion(bf16[32,2,2048]{2,0,1:T(8,128)(2,1)S(1)} %fusion.1, bf16[2,1024,2048]{2,1,0:T(8,128)(2,1)S(1)} %bitcast.84), kind=kOutput, calls=%fused_computation.12 | convolution fusion | flops 268500992 | bytes 8781824 | tf_op jit(solution)/shard_map/ref,edf->red/dot_general | solution.py:64
  41.2 0.7 pad_maximum_fusion
  42.0 0.0 reduce-scatter.2.cloned.1.call-update
  42.0 0.0 copy-start.1
  42.0 5.8 %convolution_convert_fusion = bf16[2,2048,1024]{2,1,0:T(8,128)(2,1)} fusion(bf16[32,2,2,1024]{3,0,2,1:T(8,128)(2,1)S(1)} %bitcast.87, f32[32,2,2048]{2,0,1:T(8,128)S(1)} %convolution_bitcast_fusion.1), kind=kOutput, calls=%fused_computation | convolution fusion | flops 273285120 | bytes 9043968 | tf_op jit(solution)/shard_map/ref,red->efd/dot_general | solution.py:77
  47.8 0.0 copy-start.2
  47.8 0.0 reduce-scatter.2.cloned.1.call-done
  47.8 1.7 copy.19
  49.5 6.0 %all-to-all-start.1 = ((bf16[16,2,2,1024]{3,2,1,0:T(2,128)(2,1)}), bf16[16,2,2,1024]{3,2,1,0:T(2,128)(2,1)S(1)}, u32[]{:S(2)}, u32[]{:S(2)}) async-start(bf16[16,2,2,1024]{3,2,1,0:T(2,128)(2,1)} %copy.19), calls=%async_computation.2 | async-start | bytes 262144 | tf_op jit(solution)/shard_map/all_to_all | solution.py:33
  55.5 0.2 all-reduce.2.cloned.1.call-start
  55.8 5.8 %convolution_convert_fusion.1 = bf16[2,1024,2048]{2,1,0:T(8,128)(2,1)} fusion(bf16[32,2,2048]{2,0,1:T(8,128)(2,1)S(1)} %fusion.1, bf16[32,2,2,1024]{3,0,2,1:T(8,128)(2,1)S(1)} %bitcast.88), kind=kOutput, calls=%fused_computation.1 | convolution fusion | flops 272629760 | bytes 8781824 | tf_op jit(solution)/shard_map/red,ref->edf/dot_general | solution.py:74
  61.6 1.9 all-to-all-done.1
  63.5 0.1 copy.20
  63.6 0.2 fusion.37
  63.8 0.0 copy-done.1
  63.8 0.3 convolution_bitcast_fusion.3
  64.1 0.4 fusion.22
  64.5 0.4 multiply_reduce_fusion.1
  64.8 0.9 convolution_bitcast_fusion.2
  65.8 0.0 all-reduce.2.cloned.1.call-update
  65.8 0.0 copy-done.2
  65.8 1.2 fusion.3
  67.0 122.8 %all-reduce.2.cloned.1.call-done = f32[1024,32]{0,1:T(8,128)} async-done(((f32[1024,32]{0,1:T(8,128)}), f32[1024,32]{0,1:T(8,128)}) %all-reduce.2.cloned.1.call-update) | async-done | bytes 131088 | tf_op jit(solution)/shard_map/psum | solution.py:94
  189.8 1.6 copy.40
  (4 shorter events, 0.1 us)
Async XLA Ops:
  7.2 1.0 copy-start
  7.2 40.6 %reduce-scatter.2.cloned.1.call-start = ((), (), s32[]{:S(2)}) async-start(), calls=%async_computation.3 | async-start | bytes 393216 | tf_op jit(solution)/shard_map/reduce_scatter | solution.py:25
  27.2 7.3 %slice-start = ((s8[8388608]{0:T(1024)(128)(4,1)}), s8[4194304]{0:T(1024)(128)(4,1)S(1)}, s32[]{:S(2)}) async-start(s8[8388608]{0:T(1024)(128)(4,1)} %bitcast.81), calls=%async_computation.5 | async-start | bytes 8388608
  29.4 5.1 %slice-start.1 = ((s8[8388608]{0:T(1024)(128)(4,1)}), s8[4194304]{0:T(1024)(128)(4,1)S(1)}, s32[]{:S(2)}) async-start(s8[8388608]{0:T(1024)(128)(4,1)} %bitcast.81), calls=%async_computation.6 | async-start | bytes 8388608
  29.4 9.3 %slice-start.2 = ((s8[8388608]{0:T(1024)(128)(4,1)}), s8[4194304]{0:T(1024)(128)(4,1)S(1)}, s32[]{:S(2)}) async-start(s8[8388608]{0:T(1024)(128)(4,1)} %bitcast.83), calls=%async_computation.7 | async-start | bytes 8388608
  34.5 4.2 %slice-start.3 = ((s8[8388608]{0:T(1024)(128)(4,1)}), s8[4194304]{0:T(1024)(128)(4,1)S(1)}, s32[]{:S(2)}) async-start(s8[8388608]{0:T(1024)(128)(4,1)} %bitcast.83), calls=%async_computation.8 | async-start | bytes 8388608
  42.0 21.8 %copy-start.1 = (bf16[1,256,1024]{2,1,0:T(8,128)(2,1)S(1)}, bf16[1,256,1024]{2,1,0:T(8,128)(2,1)}, u32[]{:S(2)}) copy-start(bf16[1,256,1024]{2,1,0:T(8,128)(2,1)} %param.9) | copy-start | bytes 1572868
  47.8 18.0 %copy-start.2 = (bf16[1024,32]{0,1:T(8,128)(2,1)S(1)}, bf16[1024,32]{0,1:T(8,128)(2,1)}, u32[]{:S(2)}) copy-start(bf16[1024,32]{0,1:T(8,128)(2,1)} %param.6) | copy-start | bytes 196612
  49.5 13.9 %all-to-all-start.1 = ((bf16[16,2,2,1024]{3,2,1,0:T(2,128)(2,1)}), bf16[16,2,2,1024]{3,2,1,0:T(2,128)(2,1)S(1)}, u32[]{:S(2)}, u32[]{:S(2)}) async-start(bf16[16,2,2,1024]{3,2,1,0:T(2,128)(2,1)} %copy.19), calls=%async_computation.2 | async-start | bytes 262144 | tf_op jit(solution)/shard_map/all_to_all | solution.py:33
  55.5 134.3 %all-reduce.2.cloned.1.call-start = ((), (), s32[]{:S(2)}) async-start(), calls=%async_computation.4 | async-start | bytes 262144 | tf_op jit(solution)/shard_map/psum | solution.py:94
Sparse Core Ops, SparseCore 0:
  42.1 4.9 reduce-scatter.1
  65.9 123.8 all-reduce.1
where the time goes:
time: 199 us; the launch traced here: 198 us
  waiting for transfers between devices  125 us (63%)
  matrix products  29.2 us (15%)
  blocking collectives  18.1 us (9%)
  between operations  14.2 us (7%)
  starting transfers between devices  6.26 us (3%)
  local copies, waits for them, and re-layouts  4.79 us (2%)
    psum x1, waiting for transfers between devices, per_device(): grad_param = lax.psum(local_param, ('ex', 'ey'))  123 us
    all_to_all x1, blocking collectives, route_in(): lax.all_to_all(stacked, 'ey', split_axis=2, concat_axis=0, tiled=True)  15.9 us
    all_to_all x1, starting transfers between devices, route_out(): return lax.all_to_all(summed, 'ey', split_axis=0, concat_axis=2, tiled=True)  6 us
    dot_general x1, matrix products, per_device(): jnp.einsum('ref,red->efd', hidden, slot_g, preferred_element_type=jnp.flo...  5.78 us
    dot_general x1, matrix products, per_device(): jnp.einsum('red,ref->edf', slot_x, dpre, preferred_element_type=jnp.float32)  5.78 us
    dot_general x1, matrix products, per_device(): jnp.einsum('red,edf->ref', slot_x, weight_in, preferred_element_type=jnp....  5.07 us
  transfers between devices with their start and end apart: 3, of which 2 were waited for; matrix products, arithmetic and copies ran while one was open for 6% of the time, Pallas kernels for 0%

commit v1 on v0

--- a/solution.py
+++ b/solution.py
@@ -91,7 +91,7 @@
         "ips,ds->ipd", logit_grad, slot_param, preferred_element_type=jnp.float32
     )
     local_param = jnp.einsum("ipd,ips->ds", tokens, logit_grad, preferred_element_type=jnp.float32)
-    grad_param = lax.psum(local_param, ("ex", "ey"))
+    grad_param = jnp.sum(lax.all_gather(local_param, ("ex", "ey")), axis=0)
     return (grad_tokens.astype(jnp.bfloat16), grad_param, grad_win, grad_wout)
 
 

time: 199 us -> 138 us (0.69)
  waiting for transfers between devices: 125 us -> 52 us
  blocking collectives: 18.1 us -> 32.5 us
  starting transfers between devices: 6.26 us -> 0.08 us
  local copies, waits for them, and re-layouts: 4.79 us -> 7.16 us
    psum x1 -> x0, waiting for transfers between devices: 123 us -> none  [per_device(): grad_param = lax.psum(local_param, ('ex', 'ey'))]
    all_gather x0 -> x1, waiting for transfers between devices: none -> 47 us  [per_device(): grad_param = jnp.sum(lax.all_gather(local_param, ('ex', 'ey')), axis=0)]
    all_to_all x0 -> x1, blocking collectives: none -> 14.5 us  [route_out(): return lax.all_to_all(summed, 'ey', split_axis=0, concat_axis=2, tiled=True)]
    all_to_all x1 -> x0, starting transfers between devices: 6 us -> none  [route_out(): return lax.all_to_all(summed, 'ey', split_axis=0, concat_axis=2, tiled=True)]
    reduce_scatter x1, waiting for transfers between devices: 0.01 us -> 5.05 us  [route_out(): lax.psum_scatter(term_fn(jnp.int32(0), total_rows // lax.axis_size('ex')...]
    unnamed x15, local copies, waits for them, and re-layouts: 2.6 us -> 5.65 us
  transfers between devices with their start and end apart: 3 -> 2, of which waited for: 2 -> 2; matrix products, arithmetic and copies ran while one was open for 6% -> 10% of each run, Pallas kernels for 0% -> 0%
where the time goes in v1:
time: 138 us; the launch traced here: 137 us
  waiting for transfers between devices  52 us (38%)
  blocking collectives  32.5 us (24%)
  matrix products  29.2 us (21%)
  between operations  14.2 us (10%)
  local copies, waits for them, and re-layouts  7.16 us (5%)
  other arithmetic  2.23 us (2%)
    all_gather x1, waiting for transfers between devices, per_device(): grad_param = jnp.sum(lax.all_gather(local_param, ('ex', 'ey')), axis=0)  47 us
    all_to_all x1, blocking collectives, route_in(): lax.all_to_all(stacked, 'ey', split_axis=2, concat_axis=0, tiled=True)  15.9 us
    all_to_all x1, blocking collectives, route_out(): return lax.all_to_all(summed, 'ey', split_axis=0, concat_axis=2, tiled=True)  14.5 us
    dot_general x1, matrix products, per_device(): jnp.einsum('ref,red->efd', hidden, slot_g, preferred_element_type=jnp.flo...  5.78 us
    dot_general x1, matrix products, per_device(): jnp.einsum('red,ref->edf', slot_x, dpre, preferred_element_type=jnp.float32)  5.78 us
    unnamed x15, local copies, waits for them, and re-layouts  5.65 us
    dot_general x1, matrix products, per_device(): jnp.einsum('red,edf->ref', slot_x, weight_in, preferred_element_type=jnp....  5.07 us
    reduce_scatter x1, waiting for transfers between devices, route_out(): lax.psum_scatter(term_fn(jnp.int32(0), total_rows // lax.axis_size('ex')...  5.05 us
  transfers between devices with their start and end apart: 2, of which 2 were waited for; matrix products, arithmetic and copies ran while one was open for 10% of the time, Pallas kernels for 0%

profile of v1, /device:TPU:0, one launch (start us, length us, event | category | flops | bytes accessed | tf_op | source)
XLA Modules:
  0.0 137.4 jit_solution(2617413617621177154)
XLA Ops:
  7.2 0.0 copy-start
  7.2 0.0 reduce-scatter.2.cloned.1.call-start
  7.2 1.0 copy-done
  8.2 1.2 fusion.36
  9.4 0.2 fusion.25
  9.6 0.2 fusion.6
  9.9 1.2 fusion.7
  11.1 0.1 copy.17
  11.3 15.9 %all_to_all.36 = bf16[1,2,32,1024]{3,1,0,2:T(2,128)(2,1)S(1)} all-to-all(bf16[1,2,32,1024]{3,1,0,2:T(2,128)(2,1)S(1)} %copy.17), channel_id=1, replica_groups=mesh['ex'=2,'ey'=16] {'ey'}, dimensions={2} | all-to-all | bytes 262144 | tf_op jit(solution)/shard_map/all_to_all | solution.py:20
  27.2 0.0 slice-start
  27.3 2.1 %all-gather = bf16[32,1,2,2,1024]{4,0,3,2,1:T(8,128)(2,1)S(1)} all-gather(bf16[16,1,2,2,1024]{4,0,3,2,1:T(8,128)(2,1)S(1)} %bitcast.96), channel_id=2, replica_groups=mesh['ex'=2,'ey'=16] {'ex'}, dimensions={0}, use_global_device_ids=true | all-gather | bytes 393216 | tf_op jit(solution)/shard_map/all_gather | solution.py:21
  29.4 0.0 slice-start.1
  29.4 0.0 slice-start.2
  29.4 5.1 %convolution_bitcast_fusion.1 = f32[32,2,2048]{2,0,1:T(8,128)S(1)} fusion(bf16[2,1024,2048]{2,1,0:T(8,128)(2,1)} %param.7, bf16[32,2,2,1024]{3,0,2,1:T(8,128)(2,1)S(1)} %bitcast.90), kind=kOutput, calls=%fused_computation.5 | convolution fusion | flops 268435456 | bytes 9043968 | tf_op jit(solution)/shard_map/red,edf->ref/dot_general | solution.py:52
  34.5 0.0 slice-done
  34.5 0.0 slice-done.1
  34.5 0.0 slice-start.3
  34.5 1.5 %fusion.4 = bf16[32,1,2,1024]{3,0,2,1:T(8,128)(2,1)S(1)} fusion(bf16[2,2048,1024]{2,1,0:T(8,128)(2,1)S(1)} %bitcast.87, f32[32,2,2048]{2,0,1:T(8,128)S(1)} %convolution_bitcast_fusion.1), kind=kOutput, calls=%fused_computation.12 | convolution fusion | flops 269156352 | bytes 9043968 | tf_op jit(solution)/shard_map/ref,efd->red/dot_general | solution.py:61
  36.0 0.0 copy-start.1
  36.1 2.6 %fusion.1 = bf16[32,2,2048]{2,0,1:T(8,128)(2,1)S(1)} fusion(bf16[2,2048,1024]{2,1,0:T(8,128)(2,1)S(1)} %bitcast.87, f32[32,2,2048]{2,0,1:T(8,128)S(1)} %convolution_bitcast_fusion.1, bf16[32,2,2,1024]{3,0,2,1:T(8,128)(2,1)S(1)} %bitcast.91), kind=kOutput, calls=%fused_computation.6 | convolution fusion | flops 269746176 | bytes 9306112 | tf_op jit(solution)/shard_map/red,efd->ref/dot_general | solution.py:55
  38.7 0.0 slice-done.2
  38.7 0.0 slice-done.3
  38.7 2.6 %fusion.5 = bf16[32,1,2,1024]{3,0,2,1:T(8,128)(2,1)S(1)} fusion(bf16[32,2,2048]{2,0,1:T(8,128)(2,1)S(1)} %fusion.1, bf16[2,1024,2048]{2,1,0:T(8,128)(2,1)S(1)} %bitcast.89), kind=kOutput, calls=%fused_computation.13 | convolution fusion | flops 268500992 | bytes 8781824 | tf_op jit(solution)/shard_map/ref,edf->red/dot_general | solution.py:64
  41.2 0.7 pad_maximum_fusion
  42.0 0.0 reduce-scatter.2.cloned.1.call-update
  42.0 0.0 all-gather.4.cloned.1.call-start
  42.1 5.0 %reduce-scatter.2.cloned.1.call-done = bf16[16,2,2,1024]{3,0,2,1:T(8,128)(2,1)} async-done(((bf16[32,2,2,1024]{3,0,2,1:T(8,128)(2,1)}), bf16[16,2,2,1024]{3,0,2,1:T(8,128)(2,1)}) %reduce-scatter.2.cloned.1.call-update) | async-done | bytes 131088 | tf_op jit(solution)/shard_map/reduce_scatter | solution.py:25
  47.1 1.0 copy.19
  48.2 14.5 %all_to_all.37 = bf16[16,2,2,1024]{3,2,1,0:T(2,128)(2,1)S(1)} all-to-all(bf16[16,2,2,1024]{3,2,1,0:T(2,128)(2,1)S(1)} %copy.19), channel_id=1, replica_groups=mesh['ex'=2,'ey'=16] {'ey'}, dimensions={0} | all-to-all | bytes 262144 | tf_op jit(solution)/shard_map/all_to_all | solution.py:33
  62.6 0.1 copy.20
  62.7 0.2 fusion.37
  62.9 0.0 copy-done.1
  62.9 0.3 convolution_bitcast_fusion.3
  63.2 0.4 multiply_reduce_fusion.1
  63.6 0.9 convolution_bitcast_fusion.2
  64.5 0.0 all-gather.4.cloned.1.call-update
  64.5 0.0 copy-start.2
  64.5 5.8 %convolution_convert_fusion.1 = bf16[2,1024,2048]{2,1,0:T(8,128)(2,1)} fusion(bf16[32,2,2048]{2,0,1:T(8,128)(2,1)S(1)} %fusion.1, bf16[32,2,2,1024]{3,0,2,1:T(8,128)(2,1)S(1)} %bitcast.92), kind=kOutput, calls=%fused_computation.1 | convolution fusion | flops 272629760 | bytes 8781824 | tf_op jit(solution)/shard_map/red,ref->edf/dot_general | solution.py:74
  70.3 5.8 %convolution_convert_fusion = bf16[2,2048,1024]{2,1,0:T(8,128)(2,1)} fusion(bf16[32,2,2,1024]{3,0,2,1:T(8,128)(2,1)S(1)} %bitcast.93, f32[32,2,2048]{2,0,1:T(8,128)S(1)} %convolution_bitcast_fusion.1), kind=kOutput, calls=%fused_computation | convolution fusion | flops 273285120 | bytes 9043968 | tf_op jit(solution)/shard_map/ref,red->efd/dot_general | solution.py:77
  76.1 0.4 fusion.22
  76.5 0.0 copy-done.2
  76.5 1.2 fusion.3
  77.7 47.0 %all-gather.4.cloned.1.call-done = f32[32768,32]{0,1:T(8,128)} async-done(((f32[1024,32]{0,1:T(8,128)}), f32[32768,32]{0,1:T(8,128)}) %all-gather.4.cloned.1.call-update) | async-done | bytes 4194320 | tf_op jit(solution)/shard_map/all_gather | solution.py:94
  124.7 4.6 %copy.23 = f32[4,8,32,1024]{3,2,1,0:T(8,128)S(1)} copy(f32[4,8,32,1024]{3,1,2,0:T(8,128)} %bitcast.94) | data formatting | bytes 8388608
  129.3 1.3 bitcast_reduce_fusion
  (4 shorter events, 0.1 us)
Async XLA Ops:
  7.2 1.0 copy-start
  7.2 39.9 %reduce-scatter.2.cloned.1.call-start = ((), (), s32[]{:S(2)}) async-start(), calls=%async_computation.3 | async-start | bytes 393216 | tf_op jit(solution)/shard_map/reduce_scatter | solution.py:25
  27.2 7.3 %slice-start = ((s8[8388608]{0:T(1024)(128)(4,1)}), s8[4194304]{0:T(1024)(128)(4,1)S(1)}, s32[]{:S(2)}) async-start(s8[8388608]{0:T(1024)(128)(4,1)} %bitcast.86), calls=%async_computation.5 | async-start | bytes 8388608
  29.4 5.1 %slice-start.1 = ((s8[8388608]{0:T(1024)(128)(4,1)}), s8[4194304]{0:T(1024)(128)(4,1)S(1)}, s32[]{:S(2)}) async-start(s8[8388608]{0:T(1024)(128)(4,1)} %bitcast.86), calls=%async_computation.6 | async-start | bytes 8388608
  29.4 9.3 %slice-start.2 = ((s8[8388608]{0:T(1024)(128)(4,1)}), s8[4194304]{0:T(1024)(128)(4,1)S(1)}, s32[]{:S(2)}) async-start(s8[8388608]{0:T(1024)(128)(4,1)} %bitcast.88), calls=%async_computation.7 | async-start | bytes 8388608
  34.5 4.2 %slice-start.3 = ((s8[8388608]{0:T(1024)(128)(4,1)}), s8[4194304]{0:T(1024)(128)(4,1)S(1)}, s32[]{:S(2)}) async-start(s8[8388608]{0:T(1024)(128)(4,1)} %bitcast.88), calls=%async_computation.8 | async-start | bytes 8388608
  36.0 26.9 %copy-start.1 = (bf16[1,256,1024]{2,1,0:T(8,128)(2,1)S(1)}, bf16[1,256,1024]{2,1,0:T(8,128)(2,1)}, u32[]{:S(2)}) copy-start(bf16[1,256,1024]{2,1,0:T(8,128)(2,1)} %param.9) | copy-start | bytes 1572868
  42.0 82.6 %all-gather.4.cloned.1.call-start = ((), (), s32[]{:S(2)}) async-start(), calls=%async_computation.4 | async-start | bytes 4325376 | tf_op jit(solution)/shard_map/all_gather | solution.py:94
  64.5 12.0 %copy-start.2 = (bf16[1024,32]{0,1:T(8,128)(2,1)S(1)}, bf16[1024,32]{0,1:T(8,128)(2,1)}, u32[]{:S(2)}) copy-start(bf16[1024,32]{0,1:T(8,128)(2,1)} %param.6) | copy-start | bytes 196612
Sparse Core Ops, SparseCore 0:
  42.1 4.9 reduce-scatter.1
  64.6 59.9 all-gather.3
